TPU v7x, 32 devices: a whole 2x2x4 slice. The times are simulated.
32 devices in a mesh: seq: 8 (over z, core), chan: 4 (over y, x).
Axes of the slice: x: 2, y: 2, z: 4, core: 2. Of those that a mesh axis runs over, the one named last changes fastest.
Arguments:
- hidden: bfloat16 [4096, 2560], P('seq'), may hold values from -16 to 16
- embedding: bfloat16 [4096, 2560], P('seq'), may hold values from -16 to 16
- segments: int32 [4096], replicated, may hold values from 0 to 2, never falling along the last dimension, each value on 1 to 3072 neighbouring positions
- input_norm_gain: float32 [2560], replicated, may hold values from 0.5 to 1.5
- gate_proj: bfloat16 [2560, 5120], P(None, 'chan'), may hold values from -0.125 to 0.125
- input_proj: bfloat16 [2560, 5120], P(None, 'chan'), may hold values from -0.125 to 0.125
- state_proj: bfloat16 [2560, 128], replicated, may hold values from -0.125 to 0.125
- step_proj: bfloat16 [2560, 80], P(None, 'chan'), may hold values from -1 to 1
- step_bias: float32 [80], P('chan'), may hold values from -5 to -3
- decay_log: float32 [80], P('chan'), may hold values from -8 to 1
- skip_gain: float32 [80], P('chan'), may hold values from 0.5 to 1.5
- out_gain: float32 [5120], P('chan'), may hold values from 0.5 to 1.5
- out_proj: bfloat16 [5120, 2560], P('chan'), may hold values from -0.078125 to 0.078125
- attn_gain: float32 [5120], replicated, may hold values from 0.5 to 1.5
- query_proj: bfloat16 [5120, 5120], P('seq', 'chan'), may hold values from -1 to 1
- key_proj: bfloat16 [5120, 5120], P('seq', 'chan'), may hold values from -1 to 1
- value_proj: bfloat16 [5120, 5120], P('seq', 'chan'), may hold values from -0.078125 to 0.078125
- attn_out: bfloat16 [5120, 2560], P('chan', 'seq'), may hold values from -0.078125 to 0.078125
Outputs:
- mixed: bfloat16 [4096, 2560], P('seq', 'chan')
Inputs may be any that keep to these rules, and one draw needn't show every extreme that they name: `segments`: document ids never fall along the sequence, and every document has 1 to 3072 positions.
All inputs are finite; a program needn't handle non-finite values.
Results may differ from a plain program's by a relative error of at most 0.0095.
Values may be sent and summed in bfloat16 or wider, within the bound.
A program may use at most 256 MiB of HBM per device.

v0:
```python
import jax
import jax.numpy as jnp
from jax import lax
from jax.sharding import PartitionSpec as P

N = 64
HEAD_CHANNELS = 64
AP = 160
EPSILON = 1e-05
HIGHEST = lax.Precision.HIGHEST


def carried_in(value, axis, combine, identity):
    count, here = (lax.axis_size(axis), lax.axis_index(axis))
    everything = jax.tree.map(lambda part: lax.all_gather(part, axis), value)
    start = jax.tree.map(
        lambda part, zero: jnp.broadcast_to(jnp.asarray(zero, part.dtype), part.shape),
        value,
        identity,
    )

    def lap(k, before):
        reached = k < here
        new = combine(before, jax.tree.map(lambda part: part[k], everything))
        return jax.tree.map(lambda a, b: jnp.where(reached, a, b), new, before)

    return lax.fori_loop(0, count, lap, start)


def normalize(values_in, gain_in):
    widened = values_in.astype(jnp.float32)
    factor = lax.rsqrt(jnp.mean(widened * widened, axis=-1, keepdims=True) + EPSILON)
    return (widened * factor * gain_in).astype(jnp.bfloat16)


def block_terms(inputs_x, steps_dt, rate_vec, b_rows, c_rows, doc_ids, prev_doc):
    block_len = inputs_x.shape[0]
    head_count = steps_dt.shape[1]
    per_head = inputs_x.shape[1] // head_count
    logdecay = steps_dt * rate_vec[None, :]
    running = jnp.cumsum(logdecay, axis=0)
    places = jnp.arange(block_len)
    allowed = (places[:, None] >= places[None, :]) & (doc_ids[:, None] == doc_ids[None, :])
    spread = running.T[:, :, None] - running.T[:, None, :]
    decays = jnp.exp(jnp.where(allowed[None], spread, -1e30))
    intersection = jnp.dot(c_rows, b_rows.T, precision=HIGHEST)
    scaled_x = inputs_x.reshape(block_len, head_count, per_head) * steps_dt[:, :, None]
    intra_out = jnp.einsum("hts,shp->thp", decays * intersection[None], scaled_x, precision=HIGHEST)
    final_doc = doc_ids[block_len - 1]
    keeping = (
        jnp.exp(running[block_len - 1][None, :] - running)
        * (doc_ids == final_doc).astype(jnp.float32)[:, None]
    )
    own_state = jnp.einsum("sn,shp->hnp", b_rows, scaled_x * keeping[:, :, None], precision=HIGHEST)
    through = jnp.exp(running[block_len - 1]) * (final_doc == prev_doc).astype(jnp.float32)
    entering = jnp.exp(running) * (doc_ids == prev_doc).astype(jnp.float32)[:, None]
    return (intra_out, own_state, through, entering)


def carried(c_rows, entering, state_in):
    return jnp.einsum("tn,hnp->thp", c_rows, state_in, precision=HIGHEST) * entering[:, :, None]


def compose(earlier, later):
    return (earlier[0] * later[0], later[0][:, None, None] * earlier[1] + later[1])


def local(
    hidden,
    embedding,
    segments,
    input_norm_gain,
    gate_proj,
    input_proj,
    state_proj,
    step_proj,
    step_bias,
    decay_log,
    skip_gain,
    out_gain,
    out_proj,
    attn_gain,
    query_proj,
    key_proj,
    value_proj,
    attn_out,
):
    tok_rows = hidden.shape[0]
    seq_index = lax.axis_index("seq")
    chan_index = lax.axis_index("chan")
    channel_count = lax.axis_size("chan")
    row_start = seq_index * tok_rows
    tokens_n = normalize(hidden, input_norm_gain)
    gate_z = jnp.dot(tokens_n, gate_proj, preferred_element_type=jnp.float32)
    inputs_x = jax.nn.silu(jnp.dot(tokens_n, input_proj, preferred_element_type=jnp.float32))
    b_and_c = jax.nn.silu(jnp.dot(tokens_n, state_proj, preferred_element_type=jnp.float32))
    b_rows = b_and_c[:, :N]
    c_rows = b_and_c[:, N:]
    steps_dt = jax.nn.softplus(
        jnp.dot(tokens_n, step_proj, preferred_element_type=jnp.float32) + step_bias[None, :]
    )
    rate_vec = -jnp.exp(decay_log)
    doc_ids = lax.dynamic_slice_in_dim(segments, row_start, tok_rows)
    before = lax.dynamic_slice_in_dim(segments, jnp.maximum(row_start - 1, 0), 1)[0]
    prev_doc = jnp.where(seq_index > 0, before, -1)
    intra_out, own_state, through, entering = block_terms(
        inputs_x, steps_dt, rate_vec, b_rows, c_rows, doc_ids, prev_doc
    )
    neutral = (jnp.ones_like(through), jnp.zeros_like(own_state))
    state_in = carried_in((through, own_state), "seq", compose, neutral)[1]
    mixed_y = intra_out + carried(c_rows, entering, state_in)
    y_full = (
        mixed_y.reshape(tok_rows, -1) + inputs_x * jnp.repeat(skip_gain, HEAD_CHANNELS)[None, :]
    )
    gated = y_full * jax.nn.silu(gate_z)
    squares = jnp.sum(gated * gated, axis=-1)
    weighted = (gated * out_gain[None, :]).astype(jnp.bfloat16)
    partial_value = jnp.dot(weighted, out_proj, preferred_element_type=jnp.float32)
    inner_total = gate_proj.shape[1] * channel_count
    feat_width = hidden.shape[1] // channel_count
    shares = lax.psum_scatter(partial_value, "chan", scatter_dimension=1, tiled=True)
    square_total = lax.psum(squares, "chan")
    own_cols = lax.dynamic_slice_in_dim(hidden, chan_index * feat_width, feat_width, 1)
    mixed_share = (
        own_cols.astype(jnp.float32)
        + shares * lax.rsqrt(square_total / inner_total + EPSILON)[:, None]
    ).astype(jnp.bfloat16)
    mixed_h = lax.all_gather(mixed_share, "chan", axis=1, tiled=True)
    joined = jnp.concatenate((mixed_h, embedding), axis=1)
    attention_input = normalize(joined, attn_gain)
    head_cols = query_proj.shape[1]
    pieces = (
        lax.all_gather(query_proj, "seq", axis=0, tiled=True),
        lax.all_gather(key_proj, "seq", axis=0, tiled=True),
        lax.all_gather(value_proj, "seq", axis=0, tiled=True),
    )
    query_sum, key_sum, value_sum = tuple(
        (
            jnp.dot(attention_input, piece_one, preferred_element_type=jnp.float32)
            for piece_one in pieces
        )
    )
    queries = query_sum.astype(jnp.bfloat16)
    keys_all = key_sum.astype(jnp.bfloat16)
    values_all = value_sum.astype(jnp.bfloat16)
    local_heads = head_cols // AP
    query_heads = queries.reshape(tok_rows, local_heads, AP)
    query_places = row_start + jnp.arange(tok_rows)
    scaling = AP ** (-0.5)
    row_max = jnp.full((tok_rows, local_heads), -1e30, jnp.float32)
    key_piece = lax.all_gather(keys_all, "seq", axis=0, tiled=True)
    value_piece = lax.all_gather(values_all, "seq", axis=0, tiled=True)
    piece_rows = key_piece.shape[0]
    key_heads = key_piece.reshape(piece_rows, local_heads, AP)
    value_heads = value_piece.reshape(piece_rows, local_heads, AP)
    scores = (
        jnp.einsum("qhd,khd->qhk", query_heads, key_heads, preferred_element_type=jnp.float32)
        * scaling
    )
    key_places = jnp.arange(piece_rows)
    visible = (key_places[None, :] <= query_places[:, None]) & (
        segments[None, :] == doc_ids[:, None]
    )
    scores = jnp.where(visible[:, None, :], scores, -1e30)
    new_max = jnp.maximum(row_max, jnp.max(scores, axis=-1))
    weights = jnp.exp(scores - new_max[:, :, None])
    row_sum = jnp.sum(weights, axis=-1)
    accum = jnp.einsum(
        "qhk,khd->qhd",
        weights.astype(jnp.bfloat16),
        value_heads,
        preferred_element_type=jnp.float32,
    )
    context = (accum / row_sum[:, :, None]).reshape(tok_rows, head_cols).astype(jnp.bfloat16)
    out_full = jnp.dot(
        context,
        lax.all_gather(attn_out, "seq", axis=1, tiled=True),
        preferred_element_type=jnp.float32,
    )
    out_share = lax.psum_scatter(out_full, "chan", scatter_dimension=1, tiled=True)
    own_mixed = lax.dynamic_slice_in_dim(mixed_h, chan_index * feat_width, feat_width, 1)
    return (out_share + own_mixed.astype(jnp.float32)).astype(jnp.bfloat16)


def solution(mesh):
    in_specs = (
        P("seq", None),
        P("seq", None),
        P(),
        P(),
        P(None, "chan"),
        P(None, "chan"),
        P(),
        P(None, "chan"),
        P("chan"),
        P("chan"),
        P("chan"),
        P("chan"),
        P("chan", None),
        P(),
        P("seq", "chan"),
        P("seq", "chan"),
        P("seq", "chan"),
        P("chan", "seq"),
    )
    out_specs = P("seq", "chan")
    return jax.shard_map(local, mesh=mesh, in_specs=in_specs, out_specs=out_specs, check_vma=False)
```

profile of v0, /device:TPU:0, one launch (start us, length us, event | category | flops | bytes accessed | tf_op | source)
XLA Modules:
  0.0 995.4 jit_solution(13010387898185928960)
XLA Ops:
  6.6 1.4 dynamic_slice.28
  11.3 2.3 fusion.21
  14.3 3.3 fusion.51
  17.6 1.2 reduce-window.6
  19.7 8.4 divide_multiply_fusion
  28.1 2.1 copy.52
  30.3 2.9 divide_multiply_fusion.1
  35.2 2.2 fusion.40
  40.0 13.5 %all-gather.1 = f32[8,1,20]{2,1,0:T(1,128)S(1)} all-gather(f32[1,1,20]{2,1,0:T(1,128)} %bitcast.98), channel_id=1, replica_groups=mesh['seq'=8,'chan'=4] {'seq'}, dimensions={0}, use_global_device_ids=true | all-gather | bytes 720 | tf_op jit(solution)/shard_map/all_gather | solution.py:15
  54.4 2.1 fusion.46
  56.5 40.8 %all-gather.25.cloned.1.call-done = f32[160,64,64]{2,1,0:T(8,128)} async-done(((f32[20,64,64]{2,1,0:T(8,128)}), f32[160,64,64]{2,1,0:T(8,128)}) %all-gather.25.cloned.1.call-update) | async-done | bytes 2621456 | tf_op jit(solution)/shard_map/all_gather | solution.py:15
  97.4 10.3 %while.14 = (s32[]{:T(128)}, f32[20,64,64]{2,1,0:T(8,128)S(1)}, s32[]{:T(128)}, f32[8,20]{1,0:T(8,128)S(1)}, f32[8,20,64,64]{3,2,1,0:T(8,128)}, /*index=5*/s32[]{:T(128)}, s32[]{:T(128)}) while((s32[]{:T(128)}, f32[20,64,64]{2,1,0:T(8,128)S(1)}, s32[]{:T(128)}, f32[8,20]{1,0:T(8,128)S(1)}, f32[8,20,64,64]{3,2,1,0:T(8,128)}, ...), condition=%wide.region_4.5_spmd.clone, body=%wide.region_3.4_spmd.clone.sunk | while | flops 327684 | bytes 983385 | solution.py:27
  97.6 1.2 fusion.89
  98.8 1.2 fusion.89
  100.1 1.2 fusion.89
  101.4 1.2 fusion.89
  102.6 1.2 fusion.89
  103.9 1.2 fusion.89
  105.2 1.2 fusion.89
  106.5 1.2 fusion.89
  108.8 3.3 fusion.48
  112.1 25.5 %bitcast_add_fusion.1 = f32[512,20,64]{0,2,1:T(8,128)} fusion(f32[512,20,64]{0,2,1:T(8,128)S(1)} %bitcast.89, f32[512,512]{1,0:T(8,128)} %fusion.46, f32[20,512]{1,0:T(8,128)} %bitcast.93, pred[512,512]{1,0:T(8,128)(4,1)} %fusion.43, f32[512,20,64]{0,2,1:T(8,128)S(1)} %bitcast.87, f32[512,20]{0,1:T(8,128)} %get-tuple-element.147, f32[512,20]{0,1:T(8,128)} %copy-done.6), kind=kOutput, calls=%fused_computation.38 | convolution fusion | flops 4044226560 | bytes 9297920 | tf_op jit(solution)/shard_map/hts,shp->thp/dot_general | solution.py:48
  137.6 3.4 copy.57
  141.0 8.7 multiply_reduce_fusion
  149.7 8.2 fusion.35
  158.0 9.9 psum.7
  167.9 50.3 %reduce-scatter.3.cloned.1.call-done = f32[512,640]{1,0:T(8,128)} async-done(((f32[512,2560]{1,0:T(8,128)}), f32[512,640]{1,0:T(8,128)}) %reduce-scatter.3.cloned.1.call-update) | async-done | bytes 1310736 | tf_op jit(solution)/shard_map/reduce_scatter | solution.py:121
  218.1 2.4 add_convert_fusion.1
  222.3 37.9 %all-gather.11.cloned.1.call-done = bf16[512,2560]{1,0:T(8,128)(2,1)} async-done(((bf16[512,640]{1,0:T(8,128)(2,1)}), bf16[512,2560]{1,0:T(8,128)(2,1)}) %all-gather.11.cloned.1.call-update) | async-done | bytes 2621456 | tf_op jit(solution)/shard_map/all_gather | solution.py:128
  260.2 3.8 fusion.12
  264.0 118.7 %all-gather.17.cloned.1.call-done = bf16[5120,1280]{1,0:T(8,128)(2,1)} async-done(((bf16[640,1280]{1,0:T(8,128)(2,1)}), bf16[5120,1280]{1,0:T(8,128)(2,1)}) %all-gather.17.cloned.1.call-update) | async-done | bytes 13107216 | tf_op jit(solution)/shard_map/all_gather | solution.py:134
  382.8 13.3 %convolution_convert_fusion.1 = bf16[512,1280]{1,0:T(8,128)(2,1)} fusion(bf16[5120,1280]{1,0:T(8,128)(2,1)} %all-gather.17.cloned.1.call-done, f32[5120]{0:T(1024)S(1)} %copy-done.12, f32[512]{0:T(512)S(1)} %add_rsqrt_fusion, bf16[512,2560]{1,0:T(8,128)(2,1)} %param.21, bf16[512,2560]{1,0:T(8,128)(2,1)S(1)} %copy-done.4), kind=kOutput, calls=%fused_computation.34 | convolution fusion | flops 6729891840 | bytes 19683328 | tf_op jit(solution)/shard_map/dot_general | solution.py:139
  396.1 107.4 %all-gather.13.cloned.1.call-done = bf16[5120,1280]{1,0:T(8,128)(2,1)} async-done(((bf16[640,1280]{1,0:T(8,128)(2,1)}), bf16[5120,1280]{1,0:T(8,128)(2,1)}) %all-gather.13.cloned.1.call-update) | async-done | bytes 13107216 | tf_op jit(solution)/shard_map/all_gather | solution.py:135
  503.5 13.2 %convolution_convert_fusion.2 = bf16[512,1280]{1,0:T(8,128)(2,1)} fusion(bf16[5120,1280]{1,0:T(8,128)(2,1)} %all-gather.13.cloned.1.call-done, f32[5120]{0:T(1024)S(1)} %copy-done.12, f32[512]{0:T(512)S(1)} %add_rsqrt_fusion, bf16[512,2560]{1,0:T(8,128)(2,1)} %param.21, bf16[512,2560]{1,0:T(8,128)(2,1)S(1)} %copy-done.4), kind=kOutput, calls=%fused_computation.35 | convolution fusion | flops 6729891840 | bytes 19683328 | tf_op jit(solution)/shard_map/dot_general | solution.py:139
  517.5 2.6 fusion.20
  520.2 104.0 %all-gather.21.cloned.1.call-done = bf16[5120,1280]{1,0:T(8,128)(2,1)} async-done(((bf16[640,1280]{1,0:T(8,128)(2,1)}), bf16[5120,1280]{1,0:T(8,128)(2,1)}) %all-gather.21.cloned.1.call-update) | async-done | bytes 13107216 | tf_op jit(solution)/shard_map/all_gather | solution.py:133
  624.2 13.6 %convolution_convert_fusion = bf16[512,1280]{1,0:T(8,128)(2,1)} fusion(bf16[5120,1280]{1,0:T(8,128)(2,1)} %all-gather.21.cloned.1.call-done, f32[5120]{0:T(1024)S(1)} %copy-done.12, f32[512]{0:T(512)S(1)} %add_rsqrt_fusion, bf16[512,2560]{1,0:T(8,128)(2,1)} %param.21, bf16[512,2560]{1,0:T(8,128)(2,1)} %all-gather.11.cloned.1.call-done), kind=kOutput, calls=%fused_computation.33 | convolution fusion | flops 6729891840 | bytes 19683328 | tf_op jit(solution)/shard_map/dot_general | solution.py:139
  637.8 2.4 copy.60
  640.3 83.2 %all-gather.19.cloned.1.call-done = bf16[4096,1280]{1,0:T(8,128)(2,1)} async-done(((bf16[512,1280]{1,0:T(8,128)(2,1)}), bf16[4096,1280]{1,0:T(8,128)(2,1)}) %all-gather.19.cloned.1.call-update) | async-done | bytes 10485776 | tf_op jit(solution)/shard_map/all_gather | solution.py:151
  723.4 14.5 %copy.59 = bf16[4096,1280]{0,1:T(8,128)(2,1)} copy(bf16[4096,1280]{1,0:T(8,128)(2,1)} %all-gather.19.cloned.1.call-done) | data formatting | bytes 20971520 | tf_op jit(solution)/shard_map/all_gather | solution.py:151
  737.9 84.9 %all-gather.15.cloned.1.call-done = bf16[4096,1280]{1,0:T(8,128)(2,1)} async-done(((bf16[512,1280]{1,0:T(8,128)(2,1)}), bf16[4096,1280]{1,0:T(8,128)(2,1)}) %all-gather.15.cloned.1.call-update) | async-done | bytes 10485776 | tf_op jit(solution)/shard_map/all_gather | solution.py:152
  822.8 14.5 %copy.58 = bf16[4096,1280]{0,1:T(8,128)(2,1)} copy(bf16[4096,1280]{1,0:T(8,128)(2,1)} %all-gather.15.cloned.1.call-done) | data formatting | bytes 20971520 | tf_op jit(solution)/shard_map/all_gather | solution.py:152
  837.3 28.4 %fusion.3 = (f32[512,8]{0,1:T(8,128)S(1)}, f32[8,4096,512]{2,1,0:T(8,128)}) fusion(pred[512,4096]{0,1:T(8,128)(4,1)S(1)} %fusion.20, bf16[4096,8,160]{0,2,1:T(8,128)(2,1)} %bitcast.85, bf16[512,8,160]{0,2,1:T(8,128)(2,1)} %bitcast.92), kind=kOutput, calls=%fused_computation.7 | convolution fusion | flops 5419036672 | bytes 81018880 | tf_op jit(solution)/shard_map/qhd,khd->qhk/dot_general | solution.py:157
  865.7 22.0 %fusion.1 = f32[512,8]{0,1:T(8,128)S(1)} fusion(f32[8,4096,512]{2,1,0:T(8,128)} %get-tuple-element.156, f32[512,8]{0,1:T(8,128)S(1)} %broadcast_maximum_fusion, pred[512,4096]{0,1:T(8,128)(4,1)S(1)} %fusion.20), kind=kLoop, calls=%fused_computation.5 | loop fusion | flops 67104768 | bytes 69238784 | tf_op jit(solution)/shard_map/reduce_sum | solution.py:167
  887.7 29.2 %fusion.24 = bf16[512,8,160]{0,2,1:T(8,128)(2,1)} fusion(bf16[4096,8,160]{0,2,1:T(8,128)(2,1)} %bitcast.84, f32[8,4096,512]{2,1,0:T(8,128)} %get-tuple-element.156, f32[512,8]{0,1:T(8,128)S(1)} %broadcast_maximum_fusion, pred[512,4096]{0,1:T(8,128)(4,1)S(1)} %fusion.20, f32[512,8]{0,1:T(8,128)S(1)} %fusion.1), kind=kOutput, calls=%fused_computation.37 | convolution fusion | flops 5437128704 | bytes 81035264 | tf_op jit(solution)/shard_map/qhk,khd->qhd/dot_general | solution.py:168
  916.9 9.2 fusion.73
  926.2 59.7 %reduce-scatter.5.cloned.1.call-done = f32[512,640]{1,0:T(8,128)} async-done(((f32[512,2560]{1,0:T(8,128)}), f32[512,640]{1,0:T(8,128)}) %reduce-scatter.5.cloned.1.call-update) | async-done | bytes 1310736 | tf_op jit(solution)/shard_map/reduce_scatter | solution.py:180
  985.9 2.4 add_convert_fusion
  (87 shorter events, 13.0 us)
Async XLA Ops:
  6.5 23.7 %copy-start = (bf16[2560,128]{1,0:T(8,128)(2,1)S(1)}, bf16[2560,128]{1,0:T(8,128)(2,1)}, u32[]{:S(2)}) copy-start(bf16[2560,128]{1,0:T(8,128)(2,1)} %param.26) | copy-start | bytes 1966084
  6.5 13.2 %copy-start.2 = (bf16[512,2560]{1,0:T(8,128)(2,1)S(1)}, bf16[512,2560]{1,0:T(8,128)(2,1)}, u32[]{:S(2)}) copy-start(bf16[512,2560]{1,0:T(8,128)(2,1)} %param.20) | copy-start | bytes 7864324
  6.5 13.2 %copy-start.13 = (f32[2560]{0:T(1024)S(1)}, f32[2560]{0:T(1024)}, u32[]{:S(2)}) copy-start(f32[2560]{0:T(1024)} %param.23) | copy-start | bytes 30724
  6.5 90.8 %all-gather.25.cloned.1.call-start = ((), (), s32[]{:S(2)}) async-start(), calls=%async_computation.11 | async-start | bytes 5898240 | tf_op jit(solution)/shard_map/all_gather | solution.py:15
  13.6 16.6 %copy-start.10 = (f32[512]{0:T(512)}, f32[512]{0:T(512)S(1)}, u32[]{:S(2)}) copy-start(f32[512]{0:T(512)S(1)} %add_rsqrt_fusion.2) | copy-start | bytes 6148
  30.3 2.9 copy-start.5
  30.3 3.7 copy-start.7
  34.6 0.6 copy-start.6
  38.5 179.6 %reduce-scatter.3.cloned.1.call-start = ((), (), s32[]{:S(2)}) async-start(), calls=%async_computation.2 | async-start | bytes 6553600 | tf_op jit(solution)/shard_map/reduce_scatter | solution.py:121
  137.6 3.4 copy-start.3
  137.6 3.4 copy-start.9
  137.6 3.4 copy-start.11
  137.6 3.4 copy-start.14
  141.0 8.7 copy-start.15
  157.9 102.3 %all-gather.11.cloned.1.call-start = ((), (), s32[]{:S(2)}) async-start(), calls=%async_computation.3 | async-start | bytes 3276800 | tf_op jit(solution)/shard_map/all_gather | solution.py:128
  220.5 162.2 %copy-start.12 = (f32[5120]{0:T(1024)S(1)}, f32[5120]{0:T(1024)}, u32[]{:S(2)}) copy-start(f32[5120]{0:T(1024)} %param.33) | copy-start | bytes 61444
  220.5 162.2 %all-gather.17.cloned.1.call-start = ((), (), s32[]{:S(2)}) async-start(), calls=%async_computation.6 | async-start | bytes 14745600 | tf_op jit(solution)/shard_map/all_gather | solution.py:134
  221.1 282.3 %all-gather.13.cloned.1.call-start = ((), (), s32[]{:S(2)}) async-start(), calls=%async_computation.4 | async-start | bytes 14745600 | tf_op jit(solution)/shard_map/all_gather | solution.py:135
  221.7 402.5 %all-gather.21.cloned.1.call-start = ((), (), s32[]{:S(2)}) async-start(), calls=%async_computation.8 | async-start | bytes 14745600 | tf_op jit(solution)/shard_map/all_gather | solution.py:133
  222.3 501.1 %all-gather.19.cloned.1.call-start = ((), (), s32[]{:S(2)}) async-start(), calls=%async_computation.7 | async-start | bytes 11796480 | tf_op jit(solution)/shard_map/all_gather | solution.py:151
  260.2 122.5 %copy-start.4 = (bf16[512,2560]{1,0:T(8,128)(2,1)S(1)}, bf16[512,2560]{1,0:T(8,128)(2,1)}, u32[]{:S(2)}) copy-start(bf16[512,2560]{1,0:T(8,128)(2,1)} %all-gather.11.cloned.1.call-done) | copy-start | bytes 7864324
  396.1 121.5 %copy-start.8 = (s32[4096]{0:T(1024)S(1)}, s32[4096]{0:T(1024)}, u32[]{:S(2)}) copy-start(s32[4096]{0:T(1024)} %param.22) | copy-start | bytes 49156
  396.1 426.7 %all-gather.15.cloned.1.call-start = ((), (), s32[]{:S(2)}) async-start(), calls=%async_computation.5 | async-start | bytes 11796480 | tf_op jit(solution)/shard_map/all_gather | solution.py:152
  516.7 400.2 %all-gather.23.cloned.1.call-start = ((), (), s32[]{:S(2)}) async-start(), calls=%async_computation.9 | async-start | bytes 7372800 | tf_op jit(solution)/shard_map/all_gather | solution.py:177
  517.5 468.5 %reduce-scatter.5.cloned.1.call-start = ((), (), s32[]{:S(2)}) async-start(), calls=%async_computation.10 | async-start | bytes 6553600 | tf_op jit(solution)/shard_map/reduce_scatter | solution.py:180
  916.9 71.4 %copy-start.1 = (bf16[2560,128]{1,0:T(8,128)(2,1)S(1)}, bf16[2560,128]{1,0:T(8,128)(2,1)}, u32[]{:S(2)}) copy-start(bf16[2560,128]{1,0:T(8,128)(2,1)} %param.26) | copy-start | bytes 1966084
Sparse Core Ops, SparseCore 0:
  38.6 58.6 all-gather.24
  158.0 60.0 reduce-scatter.2
  220.7 39.5 all-gather.10
  261.7 120.9 all-gather.16
  384.3 119.1 all-gather.12
  505.0 119.1 all-gather.20
  625.8 97.5 all-gather.18
  725.1 97.6 all-gather.14
  824.5 65.1 all-gather.22
  926.3 59.5 reduce-scatter.4
where the time goes:
time: 1000 us; the launch traced here: 995 us
  waiting for transfers between devices  689 us (69%)
  matrix products  171 us (17%)
  other arithmetic  51.1 us (5%)
  local copies, waits for them, and re-layouts  44.1 us (4%)
  blocking collectives  23.4 us (2%)
  between operations  15.3 us (2%)
    all_gather x1, waiting for transfers between devices, local(): lax.all_gather(key_proj, 'seq', axis=0, tiled=True)  119 us
    all_gather x1, waiting for transfers between devices, local(): lax.all_gather(value_proj, 'seq', axis=0, tiled=True)  107 us
    all_gather x1, waiting for transfers between devices, local(): lax.all_gather(query_proj, 'seq', axis=0, tiled=True)  104 us
    all_gather x1, waiting for transfers between devices, local(): value_piece = lax.all_gather(values_all, 'seq', axis=0, tiled=True)  84.9 us
    all_gather x1, waiting for transfers between devices, local(): key_piece = lax.all_gather(keys_all, 'seq', axis=0, tiled=True)  83.2 us
    reduce_scatter x1, waiting for transfers between devices, local(): lax.psum_scatter(out_full, 'chan', scatter_dimension=1, tiled=True)  59.7 us
    reduce_scatter x1, waiting for transfers between devices, local(): lax.psum_scatter(partial_value, 'chan', scatter_dimension=1, tiled=True)  50.3 us
    all_gather x1, waiting for transfers between devices, carried_in(): everything = jax.tree.map(lambda part: lax.all_gather(part, axis), value)  40.8 us
  transfers between devices with their start and end apart: 10, of which 9 were waited for; matrix products, arithmetic and copies ran while one was open for 16% of the time, Pallas kernels for 0%

commit v1 on v0

--- a/solution.py
+++ b/solution.py
@@ -148,8 +148,11 @@
     query_places = row_start + jnp.arange(tok_rows)
     scaling = AP ** (-0.5)
     row_max = jnp.full((tok_rows, local_heads), -1e30, jnp.float32)
-    key_piece = lax.all_gather(keys_all, "seq", axis=0, tiled=True)
-    value_piece = lax.all_gather(values_all, "seq", axis=0, tiled=True)
+    key_piece, value_piece = jnp.split(
+        lax.all_gather(jnp.concatenate([keys_all, values_all], axis=1), "seq", axis=0, tiled=True),
+        [keys_all.shape[1]],
+        axis=1,
+    )
     piece_rows = key_piece.shape[0]
     key_heads = key_piece.reshape(piece_rows, local_heads, AP)
     value_heads = value_piece.reshape(piece_rows, local_heads, AP)

time: 1000 us -> 1020 us (1.020)
  local copies, waits for them, and re-layouts: 44.1 us -> 59.9 us
    split x0 -> x3, local copies, waits for them, and re-layouts: none -> 44.8 us  [local(): jnp.split(lax.all_gather(jnp.concatenate([keys_all, values_all], axis=1),...]
    all_gather x2 -> x0, local copies, waits for them, and re-layouts: 29 us -> none  [the longest x1 14.5 us: local(): value_piece = lax.all_gather(values_all, 'seq', axis=0, tiled=True)]
    all_gather x1, waiting for transfers between devices: 107 us -> 119 us  [local(): lax.all_gather(value_proj, 'seq', axis=0, tiled=True)]
    all_gather x1, waiting for transfers between devices: 119 us -> 107 us  [local(): lax.all_gather(key_proj, 'seq', axis=0, tiled=True)]
    all_gather x2 -> x1, waiting for transfers between devices: 168 us -> 169 us  [local(): lax.all_gather(jnp.concatenate([keys_all, values_all], axis=1), 'seq', ax...]
  transfers between devices with their start and end apart: 10 -> 9, of which waited for: 9 -> 8; matrix products, arithmetic and copies ran while one was open for 16% -> 18% of each run, Pallas kernels for 0% -> 0%
where the time goes in v1:
time: 1020 us; the launch traced here: 1010 us
  waiting for transfers between devices  689 us (68%)
  matrix products  170 us (17%)
  local copies, waits for them, and re-layouts  59.9 us (6%)
  other arithmetic  52.3 us (5%)
  blocking collectives  23.6 us (2%)
  between operations  15 us (1%)
    all_gather x1, waiting for transfers between devices, local(): lax.all_gather(jnp.concatenate([keys_all, values_all], axis=1), 'seq', ax...  169 us
    all_gather x1, waiting for transfers between devices, local(): lax.all_gather(value_proj, 'seq', axis=0, tiled=True)  119 us
    all_gather x1, waiting for transfers between devices, local(): lax.all_gather(key_proj, 'seq', axis=0, tiled=True)  107 us
    all_gather x1, waiting for transfers between devices, local(): lax.all_gather(query_proj, 'seq', axis=0, tiled=True)  103 us
    reduce_scatter x1, waiting for transfers between devices, local(): lax.psum_scatter(out_full, 'chan', scatter_dimension=1, tiled=True)  59.6 us
    reduce_scatter x1, waiting for transfers between devices, local(): lax.psum_scatter(partial_value, 'chan', scatter_dimension=1, tiled=True)  50.2 us
    split x3, local copies, waits for them, and re-layouts, local(): jnp.split(lax.all_gather(jnp.concatenate([keys_all, values_all], axis=1),...  44.8 us
    all_gather x1, waiting for transfers between devices, carried_in(): everything = jax.tree.map(lambda part: lax.all_gather(part, axis), value)  40.7 us
  transfers between devices with their start and end apart: 9, of which 8 were waited for; matrix products, arithmetic and copies ran while one was open for 18% of the time, Pallas kernels for 0%

profile of v1, /device:TPU:0, one launch (start us, length us, event | category | flops | bytes accessed | tf_op | source)
XLA Modules:
  0.0 1011.2 jit_solution(18077290942200927381)
XLA Ops:
  6.6 1.4 dynamic_slice.28
  11.3 2.3 fusion.21
  14.3 3.3 fusion.51
  19.7 8.4 divide_multiply_fusion
  28.1 2.1 copy.52
  30.3 2.9 divide_multiply_fusion.1
  35.2 2.2 fusion.40
  40.0 13.7 %all-gather.1 = f32[8,1,20]{2,1,0:T(1,128)S(1)} all-gather(f32[1,1,20]{2,1,0:T(1,128)} %bitcast.98), channel_id=1, replica_groups=mesh['seq'=8,'chan'=4] {'seq'}, dimensions={0}, use_global_device_ids=true | all-gather | bytes 720 | tf_op jit(solution)/shard_map/all_gather | solution.py:15
  54.6 2.1 fusion.46
  56.7 40.7 %all-gather.22.cloned.1.call-done = f32[160,64,64]{2,1,0:T(8,128)} async-done(((f32[20,64,64]{2,1,0:T(8,128)}), f32[160,64,64]{2,1,0:T(8,128)}) %all-gather.22.cloned.1.call-update) | async-done | bytes 2621456 | tf_op jit(solution)/shard_map/all_gather | solution.py:15
  97.4 10.3 %while.14 = (s32[]{:T(128)}, f32[20,64,64]{2,1,0:T(8,128)S(1)}, s32[]{:T(128)}, f32[8,20]{1,0:T(8,128)S(1)}, f32[8,20,64,64]{3,2,1,0:T(8,128)}, /*index=5*/s32[]{:T(128)}, s32[]{:T(128)}) while((s32[]{:T(128)}, f32[20,64,64]{2,1,0:T(8,128)S(1)}, s32[]{:T(128)}, f32[8,20]{1,0:T(8,128)S(1)}, f32[8,20,64,64]{3,2,1,0:T(8,128)}, ...), condition=%wide.region_4.5_spmd.clone, body=%wide.region_3.4_spmd.clone.sunk | while | flops 327684 | bytes 983393 | solution.py:27
  97.6 1.2 fusion.90
  98.8 1.2 fusion.90
  100.1 1.2 fusion.90
  101.4 1.2 fusion.90
  102.7 1.2 fusion.90
  103.9 1.2 fusion.90
  105.2 1.2 fusion.90
  106.5 1.2 fusion.90
  108.8 3.3 fusion.48
  112.1 25.5 %bitcast_add_fusion.1 = f32[512,20,64]{0,2,1:T(8,128)} fusion(f32[512,20,64]{0,2,1:T(8,128)S(1)} %bitcast.89, f32[512,512]{1,0:T(8,128)} %fusion.46, f32[20,512]{1,0:T(8,128)} %bitcast.93, pred[512,512]{1,0:T(8,128)(4,1)} %fusion.43, f32[512,20,64]{0,2,1:T(8,128)S(1)} %bitcast.87, f32[512,20]{0,1:T(8,128)} %get-tuple-element.149, f32[512,20]{0,1:T(8,128)} %copy-done.7), kind=kOutput, calls=%fused_computation.39 | convolution fusion | flops 4044226560 | bytes 9297920 | tf_op jit(solution)/shard_map/hts,shp->thp/dot_general | solution.py:48
  137.6 3.4 copy.57
  141.0 8.7 multiply_reduce_fusion
  149.7 8.2 fusion.35
  158.0 9.9 psum.7
  167.9 50.2 %reduce-scatter.3.cloned.1.call-done = f32[512,640]{1,0:T(8,128)} async-done(((f32[512,2560]{1,0:T(8,128)}), f32[512,640]{1,0:T(8,128)}) %reduce-scatter.3.cloned.1.call-update) | async-done | bytes 1310736 | tf_op jit(solution)/shard_map/reduce_scatter | solution.py:121
  218.1 2.4 add_convert_fusion.1
  222.4 37.9 %all-gather.10.cloned.1.call-done = bf16[512,2560]{1,0:T(8,128)(2,1)} async-done(((bf16[512,640]{1,0:T(8,128)(2,1)}), bf16[512,2560]{1,0:T(8,128)(2,1)}) %all-gather.10.cloned.1.call-update) | async-done | bytes 2621456 | tf_op jit(solution)/shard_map/all_gather | solution.py:128
  260.2 3.8 fusion.12
  264.0 118.7 %all-gather.14.cloned.1.call-done = bf16[5120,1280]{1,0:T(8,128)(2,1)} async-done(((bf16[640,1280]{1,0:T(8,128)(2,1)}), bf16[5120,1280]{1,0:T(8,128)(2,1)}) %all-gather.14.cloned.1.call-update) | async-done | bytes 13107216 | tf_op jit(solution)/shard_map/all_gather | solution.py:135
  382.8 13.2 %convolution_convert_fusion.1 = bf16[512,1280]{1,0:T(8,128)(2,1)} fusion(bf16[5120,1280]{1,0:T(8,128)(2,1)} %all-gather.14.cloned.1.call-done, f32[5120]{0:T(1024)S(1)} %copy-done.13, f32[512]{0:T(512)S(1)} %add_rsqrt_fusion, bf16[512,2560]{1,0:T(8,128)(2,1)} %param.21, bf16[512,2560]{1,0:T(8,128)(2,1)S(1)} %copy-done.4), kind=kOutput, calls=%fused_computation.34 | convolution fusion | flops 6729891840 | bytes 19683328 | tf_op jit(solution)/shard_map/dot_general | solution.py:139
  396.0 107.5 %all-gather.12.cloned.1.call-done = bf16[5120,1280]{1,0:T(8,128)(2,1)} async-done(((bf16[640,1280]{1,0:T(8,128)(2,1)}), bf16[5120,1280]{1,0:T(8,128)(2,1)}) %all-gather.12.cloned.1.call-update) | async-done | bytes 13107216 | tf_op jit(solution)/shard_map/all_gather | solution.py:134
  503.5 12.5 %convolution_convert_fusion.2 = bf16[512,1280]{1,0:T(8,128)(2,1)S(1)} fusion(bf16[5120,1280]{1,0:T(8,128)(2,1)} %all-gather.12.cloned.1.call-done, f32[5120]{0:T(1024)S(1)} %copy-done.13, f32[512]{0:T(512)S(1)} %add_rsqrt_fusion, bf16[512,2560]{1,0:T(8,128)(2,1)} %param.21, bf16[512,2560]{1,0:T(8,128)(2,1)S(1)} %copy-done.4), kind=kOutput, calls=%fused_computation.35 | convolution fusion | flops 6729891840 | bytes 19683328 | tf_op jit(solution)/shard_map/dot_general | solution.py:139
  516.0 1.7 pad_maximum_fusion.1
  518.5 2.6 fusion.20
  521.1 103.1 %all-gather.18.cloned.1.call-done = bf16[5120,1280]{1,0:T(8,128)(2,1)} async-done(((bf16[640,1280]{1,0:T(8,128)(2,1)}), bf16[5120,1280]{1,0:T(8,128)(2,1)}) %all-gather.18.cloned.1.call-update) | async-done | bytes 13107216 | tf_op jit(solution)/shard_map/all_gather | solution.py:133
  624.2 13.6 %convolution_convert_fusion = bf16[512,1280]{1,0:T(8,128)(2,1)} fusion(bf16[5120,1280]{1,0:T(8,128)(2,1)} %all-gather.18.cloned.1.call-done, f32[5120]{0:T(1024)S(1)} %copy-done.13, f32[512]{0:T(512)S(1)} %add_rsqrt_fusion, bf16[512,2560]{1,0:T(8,128)(2,1)} %param.21, bf16[512,2560]{1,0:T(8,128)(2,1)} %all-gather.10.cloned.1.call-done), kind=kOutput, calls=%fused_computation.33 | convolution fusion | flops 6729891840 | bytes 19683328 | tf_op jit(solution)/shard_map/dot_general | solution.py:139
  637.9 2.5 copy.60
  640.3 169.2 %all-gather.16.cloned.1.call-done = bf16[4096,2560]{1,0:T(8,128)(2,1)} async-done(((bf16[512,2560]{1,0:T(8,128)(2,1)}), bf16[4096,2560]{1,0:T(8,128)(2,1)}) %all-gather.16.cloned.1.call-update) | async-done | bytes 20971536 | tf_op jit(solution)/shard_map/all_gather | solution.py:152
  809.5 16.1 %fusion.73 = (bf16[4096,1280]{1,0:T(8,128)(2,1)}, bf16[4096,1280]{1,0:T(8,128)(2,1)}) fusion(bf16[4096,2560]{1,0:T(8,128)(2,1)} %all-gather.16.cloned.1.call-done), kind=kLoop, calls=%fused_computation.96 | loop fusion | bytes 41943040 | tf_op jit(solution)/shard_map/split | solution.py:151
  825.6 14.3 %copy.58 = bf16[4096,1280]{0,1:T(8,128)(2,1)} copy(bf16[4096,1280]{1,0:T(8,128)(2,1)} %get-tuple-element.148) | data formatting | bytes 20971520 | tf_op jit(solution)/shard_map/split | solution.py:151
  839.9 14.4 %copy.59 = bf16[4096,1280]{0,1:T(8,128)(2,1)} copy(bf16[4096,1280]{1,0:T(8,128)(2,1)} %get-tuple-element.147) | data formatting | bytes 20971520 | tf_op jit(solution)/shard_map/split | solution.py:151
  854.3 28.1 %fusion.3 = (f32[512,8]{0,1:T(8,128)S(1)}, f32[8,4096,512]{2,1,0:T(8,128)}) fusion(pred[512,4096]{0,1:T(8,128)(4,1)S(1)} %fusion.20, bf16[4096,8,160]{0,2,1:T(8,128)(2,1)} %bitcast.85, bf16[512,8,160]{0,2,1:T(8,128)(2,1)} %bitcast.92), kind=kOutput, calls=%fused_computation.7 | convolution fusion | flops 5419036672 | bytes 81018880 | tf_op jit(solution)/shard_map/qhd,khd->qhk/dot_general | solution.py:160
  882.4 21.5 %fusion.1 = f32[512,8]{0,1:T(8,128)S(1)} fusion(f32[8,4096,512]{2,1,0:T(8,128)} %get-tuple-element.158, f32[512,8]{0,1:T(8,128)S(1)} %broadcast_maximum_fusion, pred[512,4096]{0,1:T(8,128)(4,1)S(1)} %fusion.20), kind=kLoop, calls=%fused_computation.5 | loop fusion | flops 67104768 | bytes 69238784 | tf_op jit(solution)/shard_map/reduce_sum | solution.py:170
  903.9 29.2 %fusion.24 = bf16[512,8,160]{0,2,1:T(8,128)(2,1)} fusion(bf16[4096,8,160]{0,2,1:T(8,128)(2,1)} %bitcast.84, f32[8,4096,512]{2,1,0:T(8,128)} %get-tuple-element.158, f32[512,8]{0,1:T(8,128)S(1)} %broadcast_maximum_fusion, pred[512,4096]{0,1:T(8,128)(4,1)S(1)} %fusion.20, f32[512,8]{0,1:T(8,128)S(1)} %fusion.1), kind=kOutput, calls=%fused_computation.38 | convolution fusion | flops 5437128704 | bytes 81035264 | tf_op jit(solution)/shard_map/qhk,khd->qhd/dot_general | solution.py:171
  933.1 9.2 fusion.74
  942.4 59.6 %reduce-scatter.5.cloned.1.call-done = f32[512,640]{1,0:T(8,128)} async-done(((f32[512,2560]{1,0:T(8,128)}), f32[512,640]{1,0:T(8,128)}) %reduce-scatter.5.cloned.1.call-update) | async-done | bytes 1310736 | tf_op jit(solution)/shard_map/reduce_scatter | solution.py:183
  1002.0 2.4 add_convert_fusion
  (88 shorter events, 14.1 us)
Async XLA Ops:
  6.5 23.8 %copy-start = (bf16[2560,128]{1,0:T(8,128)(2,1)S(1)}, bf16[2560,128]{1,0:T(8,128)(2,1)}, u32[]{:S(2)}) copy-start(bf16[2560,128]{1,0:T(8,128)(2,1)} %param.26) | copy-start | bytes 1966084
  6.5 13.2 %copy-start.2 = (bf16[512,2560]{1,0:T(8,128)(2,1)S(1)}, bf16[512,2560]{1,0:T(8,128)(2,1)}, u32[]{:S(2)}) copy-start(bf16[512,2560]{1,0:T(8,128)(2,1)} %param.20) | copy-start | bytes 7864324
  6.5 13.2 %copy-start.14 = (f32[2560]{0:T(1024)S(1)}, f32[2560]{0:T(1024)}, u32[]{:S(2)}) copy-start(f32[2560]{0:T(1024)} %param.23) | copy-start | bytes 30724
  6.5 90.8 %all-gather.22.cloned.1.call-start = ((), (), s32[]{:S(2)}) async-start(), calls=%async_computation.10 | async-start | bytes 5898240 | tf_op jit(solution)/shard_map/all_gather | solution.py:15
  13.6 16.6 %copy-start.11 = (f32[512]{0:T(512)}, f32[512]{0:T(512)S(1)}, u32[]{:S(2)}) copy-start(f32[512]{0:T(512)S(1)} %add_rsqrt_fusion.2) | copy-start | bytes 6148
  30.3 2.9 copy-start.6
  30.3 3.6 copy-start.8
  34.6 0.6 copy-start.7
  38.5 179.6 %reduce-scatter.3.cloned.1.call-start = ((), (), s32[]{:S(2)}) async-start(), calls=%async_computation.2 | async-start | bytes 6553600 | tf_op jit(solution)/shard_map/reduce_scatter | solution.py:121
  137.6 3.4 copy-start.3
  137.6 3.4 copy-start.10
  137.6 3.4 copy-start.12
  137.6 3.4 copy-start.15
  141.0 8.7 copy-start.16
  157.9 102.3 %all-gather.10.cloned.1.call-start = ((), (), s32[]{:S(2)}) async-start(), calls=%async_computation.3 | async-start | bytes 3276800 | tf_op jit(solution)/shard_map/all_gather | solution.py:128
  220.5 162.2 %copy-start.13 = (f32[5120]{0:T(1024)S(1)}, f32[5120]{0:T(1024)}, u32[]{:S(2)}) copy-start(f32[5120]{0:T(1024)} %param.33) | copy-start | bytes 61444
  220.6 162.2 %all-gather.14.cloned.1.call-start = ((), (), s32[]{:S(2)}) async-start(), calls=%async_computation.5 | async-start | bytes 14745600 | tf_op jit(solution)/shard_map/all_gather | solution.py:135
  221.1 282.3 %all-gather.12.cloned.1.call-start = ((), (), s32[]{:S(2)}) async-start(), calls=%async_computation.4 | async-start | bytes 14745600 | tf_op jit(solution)/shard_map/all_gather | solution.py:134
  221.7 402.5 %all-gather.18.cloned.1.call-start = ((), (), s32[]{:S(2)}) async-start(), calls=%async_computation.7 | async-start | bytes 14745600 | tf_op jit(solution)/shard_map/all_gather | solution.py:133
  222.3 587.2 %all-gather.16.cloned.1.call-start = ((), (), s32[]{:S(2)}) async-start(), calls=%async_computation.6 | async-start | bytes 23592960 | tf_op jit(solution)/shard_map/all_gather | solution.py:152
  260.2 122.5 %copy-start.4 = (bf16[512,2560]{1,0:T(8,128)(2,1)S(1)}, bf16[512,2560]{1,0:T(8,128)(2,1)}, u32[]{:S(2)}) copy-start(bf16[512,2560]{1,0:T(8,128)(2,1)} %all-gather.10.cloned.1.call-done) | copy-start | bytes 7864324
  503.5 12.5 %copy-start.5 = (bf16[512,1280]{1,0:T(8,128)(2,1)S(1)}, bf16[512,1280]{1,0:T(8,128)(2,1)}, u32[]{:S(2)}) copy-start(bf16[512,1280]{1,0:T(8,128)(2,1)} %convolution_convert_fusion.1) | copy-start | bytes 3932164
  516.0 2.5 copy-start.9
  517.7 415.4 %all-gather.20.cloned.1.call-start = ((), (), s32[]{:S(2)}) async-start(), calls=%async_computation.8 | async-start | bytes 7372800 | tf_op jit(solution)/shard_map/all_gather | solution.py:180
  518.4 483.6 %reduce-scatter.5.cloned.1.call-start = ((), (), s32[]{:S(2)}) async-start(), calls=%async_computation.9 | async-start | bytes 6553600 | tf_op jit(solution)/shard_map/reduce_scatter | solution.py:183
  933.1 71.3 %copy-start.1 = (bf16[2560,128]{1,0:T(8,128)(2,1)S(1)}, bf16[2560,128]{1,0:T(8,128)(2,1)}, u32[]{:S(2)}) copy-start(bf16[2560,128]{1,0:T(8,128)(2,1)} %param.26) | copy-start | bytes 1966084
Sparse Core Ops, SparseCore 0:
  38.6 58.7 all-gather.21
  158.0 60.0 reduce-scatter.2
  220.7 39.5 all-gather.9
  261.7 120.9 all-gather.13
  384.3 119.1 all-gather.11
  505.0 119.1 all-gather.17
  625.8 183.6 all-gather.15
  811.2 65.0 all-gather.19
  942.5 59.4 reduce-scatter.4
